TPU v7x, 32 devices: a whole 2x2x4 slice. The times are simulated.
32 devices in a mesh: scan: 2 (over x), tile: 16 (over z, y, core).
Axes of the slice: x: 2, y: 2, z: 4, core: 2. Of those that a mesh axis runs over, the one named last changes fastest.
Arguments:
- slices: float32 [4, 2, 1024, 1024], P(None, None, ('scan', 'tile')), parts along dimension 2, may hold values from -4 to 4
- probe_modes: float32 [4, 2, 128, 128], P('scan'), parts along dimension 0, may hold values from -4 to 4
- row_offset: int32 [128], P(('scan', 'tile')), parts along dimension 0, may hold values from 0 to 31, as said below
- col_offset: int32 [128], P(('scan', 'tile')), parts along dimension 0, may hold values from 0 to 1023
- amplitude: float32 [128, 128, 128], P(('scan', 'tile')), parts along dimension 0, may hold values from 0.5 to 3
Outputs:
- slice_grad: float32 [4, 2, 1024, 1024], P(None, None, ('scan', 'tile')), parts along dimension 2
- probe_grad: float32 [4, 2, 128, 128], P('scan'), parts along dimension 0
There are 2 independent parts, one for each index of `scan`. A program takes and returns all parts, laid end to end along the dimension named above; each array names one. Nothing has to cross between parts.
Inputs may be any that keep to these rules, and one draw needn't show every extreme that they name: Window w starts 32 * (w // 4) + row_offset[w] rows down the object; the largest value is taken by some window in every draw.
All inputs are finite; a program needn't handle non-finite values.
Results may differ from a plain program's by a relative error of at most 0.0003.
Values sent between devices are 32-bit elements; how exact they have to be, the bound alone decides.
A program may use at most 128 MiB of HBM per device.

v0:
```python
import math
import jax
import jax.numpy as jnp
from jax import lax
from jax.sharding import PartitionSpec as P

INTENSITY_SHIFT = 0.5
FRESNEL = 0.75


def from_behind(value, axis, steps):
    count = lax.axis_size(axis)
    pairs = [(source, (source + steps) % count) for source in range(count)]
    return lax.ppermute(value, axis, pairs)


def dft_tables(window_side):
    steps_idx = jnp.arange(window_side, dtype=jnp.int32)
    product = steps_idx[:, None] * steps_idx[None, :] % window_side
    angles = product.astype(jnp.float32) * (-2.0 * math.pi / window_side)
    scale = 1.0 / math.sqrt(window_side)
    return (jnp.cos(angles) * scale, jnp.sin(angles) * scale)


def fresnel_kernel(window_side):
    steps_idx = jnp.arange(window_side, dtype=jnp.int32)
    freqs = (steps_idx + window_side // 2) % window_side - window_side // 2
    radius = (freqs[:, None] * freqs[:, None] + freqs[None, :] * freqs[None, :]).astype(jnp.float32)
    phase = radius * (-math.pi * FRESNEL / (window_side / 2.0) ** 2)
    return (jnp.cos(phase), jnp.sin(phase))


def left_apply(mat_real, mat_imag, wave_real, wave_imag):

    def product(matrix, field):
        return jnp.einsum("jk,mkl->mjl", matrix, field, precision=lax.Precision.HIGHEST)

    return (
        product(mat_real, wave_real) - product(mat_imag, wave_imag),
        product(mat_real, wave_imag) + product(mat_imag, wave_real),
    )


def right_apply(wave_real, wave_imag, mat_real, mat_imag):

    def product(field, matrix):
        return jnp.einsum("mjk,kl->mjl", field, matrix, precision=lax.Precision.HIGHEST)

    return (
        product(wave_real, mat_real) - product(wave_imag, mat_imag),
        product(wave_imag, mat_real) + product(wave_real, mat_imag),
    )


def transform(wave_real, wave_imag, mat_real, mat_imag):
    half_real, half_imag = left_apply(mat_real, mat_imag, wave_real, wave_imag)
    return right_apply(half_real, half_imag, mat_real, mat_imag)


def propagate(wave_real, wave_imag, tables):
    cos_table, sin_table, kernel_real, kernel_imag = tables
    spec_real, spec_imag = transform(wave_real, wave_imag, cos_table, sin_table)
    moved_real = spec_real * kernel_real - spec_imag * kernel_imag
    moved_imag = spec_real * kernel_imag + spec_imag * kernel_real
    return transform(moved_real, moved_imag, cos_table, -sin_table)


def window_loss(crops, probe_modes, measured, tables):
    cos_table, sin_table = (tables[0], tables[1])
    wave_real = probe_modes[:, 0]
    wave_imag = probe_modes[:, 1]
    slice_count = crops.shape[0]
    exit_real = wave_real
    exit_imag = wave_imag
    for depth_index in range(slice_count):
        trans_real = crops[depth_index, 0]
        trans_imag = crops[depth_index, 1]
        exit_real = trans_real * wave_real - trans_imag * wave_imag
        exit_imag = trans_real * wave_imag + trans_imag * wave_real
        if depth_index + 1 < slice_count:
            wave_real, wave_imag = propagate(exit_real, exit_imag, tables)
    far_real, far_imag = transform(exit_real, exit_imag, cos_table, sin_table)
    intensity = jnp.sum(far_real * far_real + far_imag * far_imag, axis=0)
    modelled = jnp.sqrt(intensity + INTENSITY_SHIFT)
    return 0.5 * jnp.sum((modelled - measured) ** 2)


def window_grads(crops, probe_modes, measured, tables):
    return jax.grad(window_loss, argnums=(0, 1))(crops, probe_modes, measured, tables)


def on_device(slices, probe_modes, row_offset, col_offset, amplitude):
    window_side = probe_modes.shape[-1]
    slice_count = slices.shape[0]
    rows_here = slices.shape[2]
    cols_here = slices.shape[3]
    upper_count = (window_side - 2) // rows_here + 1
    cos_table, sin_table = dft_tables(window_side)
    kernel_real, kernel_imag = fresnel_kernel(window_side)
    tables = (cos_table, sin_table, kernel_real, kernel_imag)
    pieces = [slices]
    moving = slices
    for offset in range(upper_count):
        moving = from_behind(moving, "tile", -1)
        pieces.append(moving)
    extended = jnp.concatenate(pieces, axis=2)[:, :, : rows_here + window_side - 1]
    extended = jnp.concatenate([extended, extended[:, :, :, : window_side - 1]], axis=3)
    anchor = jnp.zeros((), jnp.int32)
    crop_shape = (slice_count, 2, window_side, window_side)

    def one_window(row_start, col_start, measured):
        corner = (anchor, anchor, row_start, col_start)
        crops = lax.dynamic_slice(extended, corner, crop_shape)
        return window_grads(crops, probe_modes, measured, tables)

    crop_grads, probe_terms = jax.vmap(one_window)(row_offset, col_offset, amplitude)

    def add_window(window_index, gradient_buffer):
        corner = (anchor, anchor, row_offset[window_index], col_offset[window_index])
        current = lax.dynamic_slice(gradient_buffer, corner, crop_shape)
        return lax.dynamic_update_slice(gradient_buffer, current + crop_grads[window_index], corner)

    gradient_buffer = lax.fori_loop(
        0, row_offset.shape[0], add_window, jnp.zeros(extended.shape, jnp.float32)
    )
    folded = (
        gradient_buffer[:, :, :, :cols_here]
        .at[:, :, :, : window_side - 1]
        .add(gradient_buffer[:, :, :, cols_here:])
    )
    pad_rows = (upper_count + 1) * rows_here - folded.shape[2]
    padded = jnp.pad(folded, ((0, 0), (0, 0), (0, pad_rows), (0, 0)))
    shares = [
        padded[:, :, offset * rows_here : (offset + 1) * rows_here]
        for offset in range(upper_count + 1)
    ]
    own_grad = shares[0]
    for offset in range(1, upper_count + 1):
        own_grad = own_grad + from_behind(shares[offset], "tile", offset)
    probe_grad = lax.psum(jnp.sum(probe_terms, axis=0), "tile")
    return (own_grad, probe_grad)


def solution(mesh):
    placed = (
        P(None, None, ("scan", "tile"), None),
        P("scan", None, None, None),
        P(("scan", "tile")),
        P(("scan", "tile")),
        P(("scan", "tile"), None, None),
    )
    return jax.shard_map(
        on_device,
        mesh=mesh,
        in_specs=placed,
        out_specs=(P(None, None, ("scan", "tile"), None), P("scan", None, None, None)),
        check_vma=False,
    )
```

profile of v0, /device:TPU:0, one launch (start us, length us, event | category | flops | bytes accessed | tf_op | source)
XLA Modules:
  0.0 459.7 jit_solution(3375297501975912838)
XLA Ops:
  7.2 5.5 %collective-permute-start = (f32[4,2,32,1024]{3,2,1,0:T(8,128)}, f32[4,2,32,1024]{3,2,1,0:T(8,128)S(1)}, u32[]{:S(2)}, u32[]{:S(2)}) collective-permute-start(f32[4,2,32,1024]{3,2,1,0:T(8,128)} %param.9), channel_id=1, source_target_pairs={{0,15},{1,0},{2,1},{3,2},{4,3},{5,4},{6,5},{7,6},{8,7},{9,8},{10,9... | collective-permute-start | bytes 3145736 | tf_op jit(solution)/shard_map/ppermute | solution.py:14
  12.7 12.6 %collective-permute-done = f32[4,2,32,1024]{3,2,1,0:T(8,128)S(1)} collective-permute-done((f32[4,2,32,1024]{3,2,1,0:T(8,128)}, f32[4,2,32,1024]{3,2,1,0:T(8,128)S(1)}, u32[]{:S(2)}, u32[]{:S(2)}) %collective-permute-start) | collective-permute-done | bytes 1048608 | tf_op jit(solution)/shard_map/ppermute | solution.py:14
  25.4 4.5 collective-permute-start.1
  29.9 12.3 %collective-permute-done.1 = f32[4,2,32,1024]{3,2,1,0:T(8,128)S(1)} collective-permute-done((f32[4,2,32,1024]{3,2,1,0:T(8,128)S(1)}, f32[4,2,32,1024]{3,2,1,0:T(8,128)S(1)}, u32[]{:S(2)}, u32[]{:S(2)}) %collective-permute-start.1) | collective-permute-done | bytes 1048608 | tf_op jit(solution)/shard_map/ppermute | solution.py:14
  42.2 4.6 %collective-permute-start.2 = (f32[4,2,32,1024]{3,2,1,0:T(8,128)S(1)}, f32[4,2,32,1024]{3,2,1,0:T(8,128)S(1)}, u32[]{:S(2)}, u32[]{:S(2)}) collective-permute-start(f32[4,2,32,1024]{3,2,1,0:T(8,128)S(1)} %collective-permute-done.1), channel_id=1, source_target_pairs={{0,15},{1,0},{2,1},{3,2},{4,3},{5,4},{6,5},{7,6},{8,7},{9,8},{10,9... | collective-permute-start | bytes 3145736 | tf_op jit(solution)/shard_map/ppermute | solution.py:14
  49.1 10.0 %collective-permute-done.2 = f32[4,2,32,1024]{3,2,1,0:T(8,128)S(1)} collective-permute-done((f32[4,2,32,1024]{3,2,1,0:T(8,128)S(1)}, f32[4,2,32,1024]{3,2,1,0:T(8,128)S(1)}, u32[]{:S(2)}, u32[]{:S(2)}) %collective-permute-start.2) | collective-permute-done | bytes 1048608 | tf_op jit(solution)/shard_map/ppermute | solution.py:14
  59.1 4.6 %collective-permute-start.3 = (f32[4,2,32,1024]{3,2,1,0:T(8,128)S(1)}, f32[4,2,32,1024]{3,2,1,0:T(8,128)}, u32[]{:S(2)}, u32[]{:S(2)}) collective-permute-start(f32[4,2,32,1024]{3,2,1,0:T(8,128)S(1)} %collective-permute-done.2), channel_id=1, source_target_pairs={{0,15},{1,0},{2,1},{3,2},{4,3},{5,4},{6,5},{7,6},{8,7},{9,8},{10,9... | collective-permute-start | bytes 3145736 | tf_op jit(solution)/shard_map/ppermute | solution.py:14
  64.6 1.3 constant_dynamic-update-slice_fusion.4
  67.2 8.8 %collective-permute-done.3 = f32[4,2,32,1024]{3,2,1,0:T(8,128)} collective-permute-done((f32[4,2,32,1024]{3,2,1,0:T(8,128)S(1)}, f32[4,2,32,1024]{3,2,1,0:T(8,128)}, u32[]{:S(2)}, u32[]{:S(2)}) %collective-permute-start.3) | collective-permute-done | bytes 1048608 | tf_op jit(solution)/shard_map/ppermute | solution.py:14
  76.0 1.3 constant_dynamic-update-slice_fusion
  77.4 3.2 pad_maximum_fusion
  80.6 17.3 %while.16 = (s32[]{:T(128)}, f32[4,2,159,1151]{3,2,1,0:T(8,128)}, s32[4,4]{1,0:T(4,128)S(1)}, f32[4,4,2,128,128]{4,3,2,1,0:T(8,128)}, s32[]{:T(128)}) while((s32[]{:T(128)}, f32[4,2,159,1151]{3,2,1,0:T(8,128)}, s32[4,4]{1,0:T(4,128)S(1)}, f32[4,4,2,128,128]{4,3,2,1,0:T(8,128)}, s32[]{:T(128)}) %tuple.92), condition=%wide.while_cond.1, body=%wide.while_body.1.sunk | while | flops 2 | bytes 1050225 | solution.py:113
  81.3 3.6 bitcast_dynamic-update-slice_fusion.2
  85.5 3.6 bitcast_dynamic-update-slice_fusion.2
  89.8 3.6 bitcast_dynamic-update-slice_fusion.2
  94.1 3.6 bitcast_dynamic-update-slice_fusion.2
  97.9 1.7 slice_bitcast_fusion.7
  110.1 1.4 fusion.38
  112.7 1.2 fusion.39
  122.1 1.6 fusion.36
  129.5 1.2 fusion.34
  131.9 1.2 fusion.35
  134.2 1.3 convolution_add_fusion.34
  146.1 1.4 fusion.88
  148.7 1.2 fusion.30
  158.1 1.6 fusion.29
  185.7 1.9 multiply_reduce_fusion.10
  196.2 1.3 fusion.11
  200.9 2.0 multiply_reduce_fusion.6
  216.7 2.2 add_bitcast_fusion.1
  222.3 1.2 add_bitcast_fusion.6
  225.9 3.0 broadcast_in_dim.12
  228.9 54.8 %while.15 = (s32[]{:T(128)}, f32[4,2,159,1151]{3,2,1,0:T(8,128)}, s32[4]{0:T(128)S(1)}, s32[4]{0:T(128)S(1)}, f32[4,4,2,128,128]{4,3,0,2,1:T(8,128)S(1)}, /*index=5*/s32[]{:T(128)}, s32[]{:T(128)}, s32[]{:T(128)}, s32[]{:T(128)}) while((s32[]{:T(128)}, f32[4,2,159,1151]{3,2,1,0:T(8,128)}, s32[4]{0:T(128)S(1)}, s32[4]{0:T(128)S(1)}, ...), condition=%wide.region_18.19_spmd, body=%wide.region_17.18_spmd.sunk | while | flops 131080 | bytes 2621641 | solution.py:123
  233.9 1.5 bitcast_add_fusion.2
  235.4 7.2 %dynamic_update_slice.8 = f32[4,2,159,1151]{3,2,1,0:T(8,128)} dynamic-update-slice(f32[4,2,159,1151]{3,2,1,0:T(8,128)} %get-tuple-element.289, f32[4,2,128,128]{3,2,1,0:T(8,128)S(1)} %bitcast_add_fusion.2, s32[]{:T(128)} %constant.98.clone.1..sunk, s32[]{:T(128)} %constant.98.clone.1..sunk, s32[]{:T(128)S(6)} %select_n.692, s32[]{:T(128)S(6)} %select_n.693) | dynamic-update-slice | bytes 1048580 | tf_op jit(solution)/shard_map/while/body/eval_jaxpr/dynamic_update_slice | solution.py:121
  247.7 1.5 bitcast_add_fusion.2
  249.2 7.0 %dynamic_update_slice.8 = f32[4,2,159,1151]{3,2,1,0:T(8,128)} dynamic-update-slice(f32[4,2,159,1151]{3,2,1,0:T(8,128)} %get-tuple-element.289, f32[4,2,128,128]{3,2,1,0:T(8,128)S(1)} %bitcast_add_fusion.2, s32[]{:T(128)} %constant.98.clone.1..sunk, s32[]{:T(128)} %constant.98.clone.1..sunk, s32[]{:T(128)S(6)} %select_n.692, s32[]{:T(128)S(6)} %select_n.693) | dynamic-update-slice | bytes 1048580 | tf_op jit(solution)/shard_map/while/body/eval_jaxpr/dynamic_update_slice | solution.py:121
  261.3 1.5 bitcast_add_fusion.2
  262.7 7.2 %dynamic_update_slice.8 = f32[4,2,159,1151]{3,2,1,0:T(8,128)} dynamic-update-slice(f32[4,2,159,1151]{3,2,1,0:T(8,128)} %get-tuple-element.289, f32[4,2,128,128]{3,2,1,0:T(8,128)S(1)} %bitcast_add_fusion.2, s32[]{:T(128)} %constant.98.clone.1..sunk, s32[]{:T(128)} %constant.98.clone.1..sunk, s32[]{:T(128)S(6)} %select_n.692, s32[]{:T(128)S(6)} %select_n.693) | dynamic-update-slice | bytes 1048580 | tf_op jit(solution)/shard_map/while/body/eval_jaxpr/dynamic_update_slice | solution.py:121
  275.0 1.5 bitcast_add_fusion.2
  276.5 7.2 %dynamic_update_slice.8 = f32[4,2,159,1151]{3,2,1,0:T(8,128)} dynamic-update-slice(f32[4,2,159,1151]{3,2,1,0:T(8,128)} %get-tuple-element.289, f32[4,2,128,128]{3,2,1,0:T(8,128)S(1)} %bitcast_add_fusion.2, s32[]{:T(128)} %constant.98.clone.1..sunk, s32[]{:T(128)} %constant.98.clone.1..sunk, s32[]{:T(128)S(6)} %select_n.692, s32[]{:T(128)S(6)} %select_n.693) | dynamic-update-slice | bytes 1048580 | tf_op jit(solution)/shard_map/while/body/eval_jaxpr/dynamic_update_slice | solution.py:121
  283.7 5.7 %slice.104 = f32[4,2,159,1024]{3,2,1,0:T(8,128)} slice(f32[4,2,159,1151]{3,2,1,0:T(8,128)} %get-tuple-element.108), slice={[0:4], [0:2], [0:159], [0:1024]} | slice | bytes 10420224 | tf_op jit(solution)/shard_map/slice | solution.py:127
  289.4 1.4 slice_add_fusion.1
  290.8 3.7 scatter-add.4
  294.5 4.1 fusion.846
  299.5 147.3 %all-reduce.13.cloned.1.call-done = f32[2,2,128,128]{2,3,0,1:T(8,128)} async-done(((f32[2,2,128,128]{2,3,0,1:T(8,128)}), f32[2,2,128,128]{2,3,0,1:T(8,128)}) %all-reduce.13.cloned.1.call-update) | async-done | bytes 262160 | tf_op jit(solution)/shard_map/psum | solution.py:140
  446.8 1.8 copy.344
  448.6 4.1 fusion.44
  (174 shorter events, 117.5 us)
Async XLA Ops:
  7.2 439.6 %all-reduce.13.cloned.1.call-start = ((), (), s32[]{:S(2)}) async-start(), calls=%async_computation | async-start | bytes 524288 | tf_op jit(solution)/shard_map/psum | solution.py:140
  7.2 18.2 %collective-permute-start = (f32[4,2,32,1024]{3,2,1,0:T(8,128)}, f32[4,2,32,1024]{3,2,1,0:T(8,128)S(1)}, u32[]{:S(2)}, u32[]{:S(2)}) collective-permute-start(f32[4,2,32,1024]{3,2,1,0:T(8,128)} %param.9), channel_id=1, source_target_pairs={{0,15},{1,0},{2,1},{3,2},{4,3},{5,4},{6,5},{7,6},{8,7},{9,8},{10,9... | collective-permute-start | bytes 3145736 | tf_op jit(solution)/shard_map/ppermute | solution.py:14
  25.4 16.8 %collective-permute-start.1 = (f32[4,2,32,1024]{3,2,1,0:T(8,128)S(1)}, f32[4,2,32,1024]{3,2,1,0:T(8,128)S(1)}, u32[]{:S(2)}, u32[]{:S(2)}) collective-permute-start(f32[4,2,32,1024]{3,2,1,0:T(8,128)S(1)} %collective-permute-done), channel_id=1, source_target_pairs={{0,15},{1,0},{2,1},{3,2},{4,3},{5,4},{6,5},{7,6},{8,7},{9,8},{10,9... | collective-permute-start | bytes 3145736 | tf_op jit(solution)/shard_map/ppermute | solution.py:14
  42.2 16.9 %collective-permute-start.2 = (f32[4,2,32,1024]{3,2,1,0:T(8,128)S(1)}, f32[4,2,32,1024]{3,2,1,0:T(8,128)S(1)}, u32[]{:S(2)}, u32[]{:S(2)}) collective-permute-start(f32[4,2,32,1024]{3,2,1,0:T(8,128)S(1)} %collective-permute-done.1), channel_id=1, source_target_pairs={{0,15},{1,0},{2,1},{3,2},{4,3},{5,4},{6,5},{7,6},{8,7},{9,8},{10,9... | collective-permute-start | bytes 3145736 | tf_op jit(solution)/shard_map/ppermute | solution.py:14
  59.1 16.9 %collective-permute-start.3 = (f32[4,2,32,1024]{3,2,1,0:T(8,128)S(1)}, f32[4,2,32,1024]{3,2,1,0:T(8,128)}, u32[]{:S(2)}, u32[]{:S(2)}) collective-permute-start(f32[4,2,32,1024]{3,2,1,0:T(8,128)S(1)} %collective-permute-done.2), channel_id=1, source_target_pairs={{0,15},{1,0},{2,1},{3,2},{4,3},{5,4},{6,5},{7,6},{8,7},{9,8},{10,9... | collective-permute-start | bytes 3145736 | tf_op jit(solution)/shard_map/ppermute | solution.py:14
  158.1 7.4 %copy-start.7 = (f32[4,128,128]{2,1,0:T(8,128)S(1)}, f32[4,128,128]{2,1,0:T(8,128)}, u32[]{:S(2)}) copy-start(f32[4,128,128]{2,1,0:T(8,128)} %param.13) | copy-start | bytes 786436
  218.9 4.7 %copy-start.1 = (f32[4,128,128]{2,1,0:T(8,128)S(1)}, f32[4,128,128]{2,1,0:T(8,128)}, u32[]{:S(2)}) copy-start(f32[4,128,128]{2,1,0:T(8,128)} %get-tuple-element.139) | copy-start | bytes 786436
  218.9 4.7 %copy-start.2 = (f32[4,128,128]{2,1,0:T(8,128)S(1)}, f32[4,128,128]{2,1,0:T(8,128)}, u32[]{:S(2)}) copy-start(f32[4,128,128]{2,1,0:T(8,128)} %get-tuple-element.140) | copy-start | bytes 786436
  218.9 4.7 %copy-start.3 = (f32[4,128,128]{2,1,0:T(8,128)S(1)}, f32[4,128,128]{2,1,0:T(8,128)}, u32[]{:S(2)}) copy-start(f32[4,128,128]{2,1,0:T(8,128)} %get-tuple-element.141) | copy-start | bytes 786436
  219.7 4.9 %copy-start.4 = (f32[4,128,128]{2,1,0:T(8,128)S(1)}, f32[4,128,128]{2,1,0:T(8,128)}, u32[]{:S(2)}) copy-start(f32[4,128,128]{2,1,0:T(8,128)} %copy.339) | copy-start | bytes 786436
  220.6 4.0 copy-start.5
  221.4 3.2 copy-start.6
  225.6 3.2 copy-start.8
  225.6 3.2 copy-start.9
  294.5 4.2 copy-start
  298.5 150.0 %collective-permute-start.4 = (f32[4,2,32,1024]{3,2,1,0:T(8,128)}, f32[4,2,32,1024]{3,2,1,0:T(8,128)}, u32[]{:S(2)}, u32[]{:S(2)}) collective-permute-start(f32[4,2,32,1024]{3,2,1,0:T(8,128)} %get-tuple-element.169), channel_id=1, source_target_pairs={{0,1},{1,2},{2,3},{3,4},{4,5},{5,6},{6,7},{7,8},{8,9},{9,10},{10,1... | collective-permute-start | bytes 3145736 | tf_op jit(solution)/shard_map/ppermute | solution.py:14
  298.5 150.0 %collective-permute-start.5 = (f32[4,2,32,1024]{3,2,1,0:T(8,128)}, f32[4,2,32,1024]{3,2,1,0:T(8,128)}, u32[]{:S(2)}, u32[]{:S(2)}) collective-permute-start(f32[4,2,32,1024]{3,2,1,0:T(8,128)} %get-tuple-element.172), channel_id=1, source_target_pairs={{0,2},{1,3},{2,4},{3,5},{4,6},{5,7},{6,8},{7,9},{8,10},{9,11},{10,... | collective-permute-start | bytes 3145736 | tf_op jit(solution)/shard_map/ppermute | solution.py:14
  298.5 150.0 %collective-permute-start.6 = (f32[4,2,32,1024]{3,2,1,0:T(8,128)S(1)}, f32[4,2,32,1024]{3,2,1,0:T(8,128)}, u32[]{:S(2)}, u32[]{:S(2)}) collective-permute-start(f32[4,2,32,1024]{3,2,1,0:T(8,128)S(1)} %get-tuple-element.171), channel_id=1, source_target_pairs={{0,3},{1,4},{2,5},{3,6},{4,7},{5,8},{6,9},{7,10},{8,11},{9,12},{10... | collective-permute-start | bytes 3145736 | tf_op jit(solution)/shard_map/ppermute | solution.py:14
  298.6 150.0 %collective-permute-start.7 = (f32[4,2,32,1024]{3,2,1,0:T(8,128)S(1)}, f32[4,2,32,1024]{3,2,1,0:T(8,128)}, u32[]{:S(2)}, u32[]{:S(2)}) collective-permute-start(f32[4,2,32,1024]{3,2,1,0:T(8,128)S(1)} %get-tuple-element.170), channel_id=1, source_target_pairs={{0,4},{1,5},{2,6},{3,7},{4,8},{5,9},{6,10},{7,11},{8,12},{9,13},{1... | collective-permute-start | bytes 3145736 | tf_op jit(solution)/shard_map/ppermute | solution.py:14
Sparse Core Ops, SparseCore 0:
  299.6 147.1 all-reduce.12
where the time goes:
time: 465 us; the launch traced here: 460 us
  waiting for transfers between devices  191 us (41%)
  matrix products  118 us (25%)
  local copies, waits for them, and re-layouts  78.8 us (17%)
  other arithmetic  21.3 us (5%)
  starting transfers between devices  19.4 us (4%)
  loops' own time  15.7 us (3%)
  between operations  15.3 us (3%)
    psum x1, waiting for transfers between devices, on_device(): probe_grad = lax.psum(jnp.sum(probe_terms, axis=0), 'tile')  147 us
    dot_general x56, matrix products, product(): jnp.einsum('jk,mkl->mjl', matrix, field, precision=lax.Precision.HIGHEST)  62.5 us
    dot_general x56, matrix products, product(): jnp.einsum('mjk,kl->mjl', field, matrix, precision=lax.Precision.HIGHEST)  55.6 us
    ppermute x8, waiting for transfers between devices, from_behind(): return lax.ppermute(value, axis, pairs)  43.8 us
    dynamic_update_slice x4, local copies, waits for them, and re-layouts, add_window(): lax.dynamic_update_slice(gradient_buffer, current + crop_grads[window_ind...  28.6 us
    ppermute x8, starting transfers between devices, from_behind(): return lax.ppermute(value, axis, pairs)  19.4 us
    gather x12, local copies, waits for them, and re-layouts  17.1 us
    another operation x1, loops' own time, on_device(): lax.fori_loop(0, row_offset.shape[0], add_window, jnp.zeros(extended.shap...  15.6 us
  transfers between devices with their start and end apart: 9, of which 5 were waited for; matrix products, arithmetic and copies ran while one was open for 2% of the time, Pallas kernels for 0%

commit v1 on v0

--- a/solution.py
+++ b/solution.py
@@ -137,7 +137,9 @@
     own_grad = shares[0]
     for offset in range(1, upper_count + 1):
         own_grad = own_grad + from_behind(shares[offset], "tile", offset)
-    probe_grad = lax.psum(jnp.sum(probe_terms, axis=0), "tile")
+    own = jnp.sum(probe_terms, axis=0)
+    parts = lax.all_gather(own, "tile", axis=0, tiled=False)
+    probe_grad = parts.sum(axis=0)
     return (own_grad, probe_grad)
 
 

time: 465 us -> 395 us (0.85)
  the two profiles are of different devices: /device:TPU:0 before, /device:TPU:5 now
where the time goes in v1:
time: 395 us; the launch traced here: 390 us
  waiting for transfers between devices  142 us (36%)
  matrix products  117 us (30%)
  local copies, waits for them, and re-layouts  75.4 us (19%)
  other arithmetic  21.4 us (5%)
  loops' own time  15.7 us (4%)
  between operations  15.3 us (4%)
    ppermute x8, waiting for transfers between devices, from_behind(): return lax.ppermute(value, axis, pairs)  142 us
    dot_general x56, matrix products, product(): jnp.einsum('jk,mkl->mjl', matrix, field, precision=lax.Precision.HIGHEST)  61.5 us
    dot_general x56, matrix products, product(): jnp.einsum('mjk,kl->mjl', field, matrix, precision=lax.Precision.HIGHEST)  55.6 us
    dynamic_update_slice x4, local copies, waits for them, and re-layouts, add_window(): lax.dynamic_update_slice(gradient_buffer, current + crop_grads[window_ind...  28.6 us
    gather x12, local copies, waits for them, and re-layouts  16.2 us
    another operation x1, loops' own time, on_device(): lax.fori_loop(0, row_offset.shape[0], add_window, jnp.zeros(extended.shap...  15.6 us
  transfers between devices with their start and end apart: 9, of which 8 were waited for; matrix products, arithmetic and copies ran while one was open for 18% of the time, Pallas kernels for 0%

profile of v1, /device:TPU:5, one launch (start us, length us, event | category | flops | bytes accessed | tf_op | source)
XLA Modules:
  0.0 390.3 jit_solution(15213727466732788741)
XLA Ops:
  7.9 14.7 %collective-permute-done = f32[4,2,32,1024]{3,2,1,0:T(8,128)S(1)} collective-permute-done((f32[4,2,32,1024]{3,2,1,0:T(8,128)}, f32[4,2,32,1024]{3,2,1,0:T(8,128)S(1)}, u32[]{:S(2)}, u32[]{:S(2)}) %collective-permute-start) | collective-permute-done | bytes 1048608 | tf_op jit(solution)/shard_map/ppermute | solution.py:14
  22.6 15.1 %collective-permute-done.1 = f32[4,2,32,1024]{3,2,1,0:T(8,128)S(1)} collective-permute-done((f32[4,2,32,1024]{3,2,1,0:T(8,128)S(1)}, f32[4,2,32,1024]{3,2,1,0:T(8,128)S(1)}, u32[]{:S(2)}, u32[]{:S(2)}) %collective-permute-start.1) | collective-permute-done | bytes 1048608 | tf_op jit(solution)/shard_map/ppermute | solution.py:14
  40.0 12.8 %collective-permute-done.2 = f32[4,2,32,1024]{3,2,1,0:T(8,128)S(1)} collective-permute-done((f32[4,2,32,1024]{3,2,1,0:T(8,128)S(1)}, f32[4,2,32,1024]{3,2,1,0:T(8,128)S(1)}, u32[]{:S(2)}, u32[]{:S(2)}) %collective-permute-start.2) | collective-permute-done | bytes 1048608 | tf_op jit(solution)/shard_map/ppermute | solution.py:14
  53.8 1.3 constant_dynamic-update-slice_fusion.4
  56.4 11.7 %collective-permute-done.3 = f32[4,2,32,1024]{3,2,1,0:T(8,128)} collective-permute-done((f32[4,2,32,1024]{3,2,1,0:T(8,128)S(1)}, f32[4,2,32,1024]{3,2,1,0:T(8,128)}, u32[]{:S(2)}, u32[]{:S(2)}) %collective-permute-start.3) | collective-permute-done | bytes 1048608 | tf_op jit(solution)/shard_map/ppermute | solution.py:14
  68.1 1.3 constant_dynamic-update-slice_fusion
  69.5 3.2 pad_maximum_fusion
  72.6 16.4 %while.16 = (s32[]{:T(128)}, f32[4,2,159,1151]{3,2,1,0:T(8,128)}, s32[4,4]{1,0:T(4,128)S(1)}, f32[4,4,2,128,128]{4,3,2,1,0:T(8,128)}, s32[]{:T(128)}) while((s32[]{:T(128)}, f32[4,2,159,1151]{3,2,1,0:T(8,128)}, s32[4,4]{1,0:T(4,128)S(1)}, f32[4,4,2,128,128]{4,3,2,1,0:T(8,128)}, s32[]{:T(128)}) %tuple.90), condition=%wide.while_cond.1, body=%wide.while_body.1.sunk | while | flops 2 | bytes 1050225 | solution.py:113
  73.2 3.5 bitcast_dynamic-update-slice_fusion.2
  77.3 3.5 bitcast_dynamic-update-slice_fusion.2
  81.4 3.5 bitcast_dynamic-update-slice_fusion.2
  85.4 3.5 bitcast_dynamic-update-slice_fusion.2
  89.0 1.7 slice_bitcast_fusion.7
  101.3 1.4 fusion.38
  103.9 1.2 fusion.39
  113.2 1.6 fusion.36
  120.7 1.2 fusion.34
  123.0 1.2 fusion.35
  125.4 1.3 convolution_add_fusion.34
  137.2 1.4 fusion.88
  139.8 1.2 fusion.30
  149.2 1.6 fusion.29
  176.9 1.8 multiply_reduce_fusion.10
  187.1 1.3 fusion.11
  191.9 2.0 multiply_reduce_fusion.6
  207.6 1.3 add_bitcast_fusion.1
  215.9 3.0 broadcast_in_dim.12
  218.9 54.8 %while.15 = (s32[]{:T(128)}, f32[4,2,159,1151]{3,2,1,0:T(8,128)}, s32[4]{0:T(128)S(1)}, s32[4]{0:T(128)S(1)}, f32[4,4,2,128,128]{4,3,0,2,1:T(8,128)S(1)}, /*index=5*/s32[]{:T(128)}, s32[]{:T(128)}, s32[]{:T(128)}, s32[]{:T(128)}) while((s32[]{:T(128)}, f32[4,2,159,1151]{3,2,1,0:T(8,128)}, s32[4]{0:T(128)S(1)}, s32[4]{0:T(128)S(1)}, ...), condition=%wide.region_18.19_spmd, body=%wide.region_17.18_spmd.sunk | while | flops 131080 | bytes 2621641 | solution.py:123
  223.9 1.5 bitcast_add_fusion.2
  225.4 7.3 %dynamic_update_slice.8 = f32[4,2,159,1151]{3,2,1,0:T(8,128)} dynamic-update-slice(f32[4,2,159,1151]{3,2,1,0:T(8,128)} %get-tuple-element.285, f32[4,2,128,128]{3,2,1,0:T(8,128)S(1)} %bitcast_add_fusion.2, s32[]{:T(128)} %constant.98.clone.1..sunk, s32[]{:T(128)} %constant.98.clone.1..sunk, s32[]{:T(128)S(6)} %select_n.692, s32[]{:T(128)S(6)} %select_n.693) | dynamic-update-slice | bytes 1048580 | tf_op jit(solution)/shard_map/while/body/eval_jaxpr/dynamic_update_slice | solution.py:121
  237.9 1.5 bitcast_add_fusion.2
  239.3 7.0 %dynamic_update_slice.8 = f32[4,2,159,1151]{3,2,1,0:T(8,128)} dynamic-update-slice(f32[4,2,159,1151]{3,2,1,0:T(8,128)} %get-tuple-element.285, f32[4,2,128,128]{3,2,1,0:T(8,128)S(1)} %bitcast_add_fusion.2, s32[]{:T(128)} %constant.98.clone.1..sunk, s32[]{:T(128)} %constant.98.clone.1..sunk, s32[]{:T(128)S(6)} %select_n.692, s32[]{:T(128)S(6)} %select_n.693) | dynamic-update-slice | bytes 1048580 | tf_op jit(solution)/shard_map/while/body/eval_jaxpr/dynamic_update_slice | solution.py:121
  251.4 1.5 bitcast_add_fusion.2
  253.0 7.2 %dynamic_update_slice.8 = f32[4,2,159,1151]{3,2,1,0:T(8,128)} dynamic-update-slice(f32[4,2,159,1151]{3,2,1,0:T(8,128)} %get-tuple-element.285, f32[4,2,128,128]{3,2,1,0:T(8,128)S(1)} %bitcast_add_fusion.2, s32[]{:T(128)} %constant.98.clone.1..sunk, s32[]{:T(128)} %constant.98.clone.1..sunk, s32[]{:T(128)S(6)} %select_n.692, s32[]{:T(128)S(6)} %select_n.693) | dynamic-update-slice | bytes 1048580 | tf_op jit(solution)/shard_map/while/body/eval_jaxpr/dynamic_update_slice | solution.py:121
  265.2 1.5 bitcast_add_fusion.2
  266.7 7.0 %dynamic_update_slice.8 = f32[4,2,159,1151]{3,2,1,0:T(8,128)} dynamic-update-slice(f32[4,2,159,1151]{3,2,1,0:T(8,128)} %get-tuple-element.285, f32[4,2,128,128]{3,2,1,0:T(8,128)S(1)} %bitcast_add_fusion.2, s32[]{:T(128)} %constant.98.clone.1..sunk, s32[]{:T(128)} %constant.98.clone.1..sunk, s32[]{:T(128)S(6)} %select_n.692, s32[]{:T(128)S(6)} %select_n.693) | dynamic-update-slice | bytes 1048580 | tf_op jit(solution)/shard_map/while/body/eval_jaxpr/dynamic_update_slice | solution.py:121
  273.7 5.7 %slice.104 = f32[4,2,159,1024]{3,2,1,0:T(8,128)} slice(f32[4,2,159,1151]{3,2,1,0:T(8,128)} %get-tuple-element.108), slice={[0:4], [0:2], [0:159], [0:1024]} | slice | bytes 10420224 | tf_op jit(solution)/shard_map/slice | solution.py:127
  279.5 1.4 slice_add_fusion.1
  280.8 3.7 scatter-add.4
  284.5 2.5 fusion.846
  287.2 1.4 collective-permute-start.6
  288.6 1.5 collective-permute-start.7
  290.1 19.3 %collective-permute-done.4 = f32[4,2,32,1024]{3,2,1,0:T(8,128)S(1)} collective-permute-done((f32[4,2,32,1024]{3,2,1,0:T(8,128)S(1)}, f32[4,2,32,1024]{3,2,1,0:T(8,128)S(1)}, u32[]{:S(2)}, u32[]{:S(2)}) %collective-permute-start.4) | collective-permute-done | bytes 1048608 | tf_op jit(solution)/shard_map/ppermute | solution.py:14
  309.4 22.5 %collective-permute-done.5 = f32[4,2,32,1024]{3,2,1,0:T(8,128)S(1)} collective-permute-done((f32[4,2,32,1024]{3,2,1,0:T(8,128)S(1)}, f32[4,2,32,1024]{3,2,1,0:T(8,128)S(1)}, u32[]{:S(2)}, u32[]{:S(2)}) %collective-permute-start.5) | collective-permute-done | bytes 1048608 | tf_op jit(solution)/shard_map/ppermute | solution.py:14
  331.9 22.5 %collective-permute-done.6 = f32[4,2,32,1024]{3,2,1,0:T(8,128)S(1)} collective-permute-done((f32[4,2,32,1024]{3,2,1,0:T(8,128)S(1)}, f32[4,2,32,1024]{3,2,1,0:T(8,128)S(1)}, u32[]{:S(2)}, u32[]{:S(2)}) %collective-permute-start.6) | collective-permute-done | bytes 1048608 | tf_op jit(solution)/shard_map/ppermute | solution.py:14
  354.4 23.1 %collective-permute-done.7 = f32[4,2,32,1024]{3,2,1,0:T(8,128)S(1)} collective-permute-done((f32[4,2,32,1024]{3,2,1,0:T(8,128)S(1)}, f32[4,2,32,1024]{3,2,1,0:T(8,128)S(1)}, u32[]{:S(2)}, u32[]{:S(2)}) %collective-permute-start.7) | collective-permute-done | bytes 1048608 | tf_op jit(solution)/shard_map/ppermute | solution.py:14
  377.4 2.7 fusion.44
  380.2 3.1 reduce_sum.197
  (173 shorter events, 118.2 us)
Async XLA Ops:
  7.2 373.0 %all-gather.3.cloned.1.call-start = ((), (), s32[]{:S(2)}) async-start(), calls=%async_computation | async-start | bytes 4456448 | tf_op jit(solution)/shard_map/all_gather | solution.py:141
  7.2 15.4 %collective-permute-start = (f32[4,2,32,1024]{3,2,1,0:T(8,128)}, f32[4,2,32,1024]{3,2,1,0:T(8,128)S(1)}, u32[]{:S(2)}, u32[]{:S(2)}) collective-permute-start(f32[4,2,32,1024]{3,2,1,0:T(8,128)} %param.9), channel_id=1, source_target_pairs={{0,15},{1,0},{2,1},{3,2},{4,3},{5,4},{6,5},{7,6},{8,7},{9,8},{10,9... | collective-permute-start | bytes 3145736 | tf_op jit(solution)/shard_map/ppermute | solution.py:14
  22.6 15.1 %collective-permute-start.1 = (f32[4,2,32,1024]{3,2,1,0:T(8,128)S(1)}, f32[4,2,32,1024]{3,2,1,0:T(8,128)S(1)}, u32[]{:S(2)}, u32[]{:S(2)}) collective-permute-start(f32[4,2,32,1024]{3,2,1,0:T(8,128)S(1)} %collective-permute-done), channel_id=1, source_target_pairs={{0,15},{1,0},{2,1},{3,2},{4,3},{5,4},{6,5},{7,6},{8,7},{9,8},{10,9... | collective-permute-start | bytes 3145736 | tf_op jit(solution)/shard_map/ppermute | solution.py:14
  37.7 15.1 %collective-permute-start.2 = (f32[4,2,32,1024]{3,2,1,0:T(8,128)S(1)}, f32[4,2,32,1024]{3,2,1,0:T(8,128)S(1)}, u32[]{:S(2)}, u32[]{:S(2)}) collective-permute-start(f32[4,2,32,1024]{3,2,1,0:T(8,128)S(1)} %collective-permute-done.1), channel_id=1, source_target_pairs={{0,15},{1,0},{2,1},{3,2},{4,3},{5,4},{6,5},{7,6},{8,7},{9,8},{10,9... | collective-permute-start | bytes 3145736 | tf_op jit(solution)/shard_map/ppermute | solution.py:14
  52.8 15.2 %collective-permute-start.3 = (f32[4,2,32,1024]{3,2,1,0:T(8,128)S(1)}, f32[4,2,32,1024]{3,2,1,0:T(8,128)}, u32[]{:S(2)}, u32[]{:S(2)}) collective-permute-start(f32[4,2,32,1024]{3,2,1,0:T(8,128)S(1)} %collective-permute-done.2), channel_id=1, source_target_pairs={{0,15},{1,0},{2,1},{3,2},{4,3},{5,4},{6,5},{7,6},{8,7},{9,8},{10,9... | collective-permute-start | bytes 3145736 | tf_op jit(solution)/shard_map/ppermute | solution.py:14
  149.2 7.4 %copy-start.6 = (f32[4,128,128]{2,1,0:T(8,128)S(1)}, f32[4,128,128]{2,1,0:T(8,128)}, u32[]{:S(2)}) copy-start(f32[4,128,128]{2,1,0:T(8,128)} %param.13) | copy-start | bytes 786436
  208.9 4.4 %copy-start = (f32[4,128,128]{2,1,0:T(8,128)S(1)}, f32[4,128,128]{2,1,0:T(8,128)}, u32[]{:S(2)}) copy-start(f32[4,128,128]{2,1,0:T(8,128)} %get-tuple-element.133) | copy-start | bytes 786436
  208.9 4.4 %copy-start.1 = (f32[4,128,128]{2,1,0:T(8,128)S(1)}, f32[4,128,128]{2,1,0:T(8,128)}, u32[]{:S(2)}) copy-start(f32[4,128,128]{2,1,0:T(8,128)} %get-tuple-element.134) | copy-start | bytes 786436
  209.9 3.6 copy-start.2
  210.7 3.9 copy-start.3
  211.6 3.0 copy-start.4
  212.4 2.2 copy-start.5
  215.6 3.2 copy-start.7
  215.7 3.2 copy-start.8
  287.1 22.3 %collective-permute-start.4 = (f32[4,2,32,1024]{3,2,1,0:T(8,128)S(1)}, f32[4,2,32,1024]{3,2,1,0:T(8,128)S(1)}, u32[]{:S(2)}, u32[]{:S(2)}) collective-permute-start(f32[4,2,32,1024]{3,2,1,0:T(8,128)S(1)} %get-tuple-element.165), channel_id=1, source_target_pairs={{0,1},{1,2},{2,3},{3,4},{4,5},{5,6},{6,7},{7,8},{8,9},{9,10},{10,1... | collective-permute-start | bytes 3145736 | tf_op jit(solution)/shard_map/ppermute | solution.py:14
  287.1 44.8 %collective-permute-start.5 = (f32[4,2,32,1024]{3,2,1,0:T(8,128)S(1)}, f32[4,2,32,1024]{3,2,1,0:T(8,128)S(1)}, u32[]{:S(2)}, u32[]{:S(2)}) collective-permute-start(f32[4,2,32,1024]{3,2,1,0:T(8,128)S(1)} %get-tuple-element.168), channel_id=1, source_target_pairs={{0,2},{1,3},{2,4},{3,5},{4,6},{5,7},{6,8},{7,9},{8,10},{9,11},{10,... | collective-permute-start | bytes 3145736 | tf_op jit(solution)/shard_map/ppermute | solution.py:14
  287.2 67.2 %collective-permute-start.6 = (f32[4,2,32,1024]{3,2,1,0:T(8,128)S(1)}, f32[4,2,32,1024]{3,2,1,0:T(8,128)S(1)}, u32[]{:S(2)}, u32[]{:S(2)}) collective-permute-start(f32[4,2,32,1024]{3,2,1,0:T(8,128)S(1)} %get-tuple-element.167), channel_id=1, source_target_pairs={{0,3},{1,4},{2,5},{3,6},{4,7},{5,8},{6,9},{7,10},{8,11},{9,12},{10... | collective-permute-start | bytes 3145736 | tf_op jit(solution)/shard_map/ppermute | solution.py:14
  288.6 88.8 %collective-permute-start.7 = (f32[4,2,32,1024]{3,2,1,0:T(8,128)S(1)}, f32[4,2,32,1024]{3,2,1,0:T(8,128)S(1)}, u32[]{:S(2)}, u32[]{:S(2)}) collective-permute-start(f32[4,2,32,1024]{3,2,1,0:T(8,128)S(1)} %get-tuple-element.166), channel_id=1, source_target_pairs={{0,4},{1,5},{2,6},{3,7},{4,8},{5,9},{6,10},{7,11},{8,12},{9,13},{1... | collective-permute-start | bytes 3145736 | tf_op jit(solution)/shard_map/ppermute | solution.py:14
Sparse Core Ops, SparseCore 0:
  210.0 57.7 all-gather.2
